TPU v7x, 32 devices: a whole 2x2x4 slice. The times are simulated.
32 devices in a mesh: dp: 16 (over z, y, core), query: 2 (over x).
Axes of the slice: x: 2, y: 2, z: 4, core: 2. Of those that a mesh axis runs over, the one named last changes fastest.
Arguments:
- tokens: bfloat16 [2, 32, 128, 1280], P(None, ('dp', 'query')), may hold values from -6 to 6
- out_cotangent: bfloat16 [2, 32, 128, 1280], P(None, ('dp', 'query')), may hold values from -6 to 6
- qkv_weight: bfloat16 [1280, 3840], P('dp'), may hold values from -0.15625 to 0.15625
- out_weight: bfloat16 [1280, 1280], P('dp'), may hold values from -0.625 to 0.625
- up_weight: bfloat16 [1280, 5120], P('dp'), may hold values from -0.15625 to 0.15625
- down_weight: bfloat16 [5120, 1280], P('dp'), may hold values from -0.078125 to 0.078125
- attn_gain: bfloat16 [1280], P('dp'), may hold values from 0.5 to 1.5
- ffn_gain: bfloat16 [1280], P('dp'), may hold values from 0.5 to 1.5
- up_bias: bfloat16 [5120], P('dp'), may hold values from -3 to 3
- cell_weight: bfloat16 [1280, 5120], P('dp'), may hold values from -0.15625 to 0.15625
- gene_weight: bfloat16 [1280, 5120], P('dp'), may hold values from -0.15625 to 0.15625
- decoder_bias: bfloat16 [5120], P('dp'), may hold values from -3 to 3
- readout: bfloat16 [5120], P('dp'), may hold values from -0.15625 to 0.15625
- gene_embed: bfloat16 [2, 32, 384, 1280], P(None, ('dp', 'query')), may hold values from -6 to 6
- query_cell: int32 [2, 32, 384], P(None, ('dp', 'query')), may hold values from 0 to 1
- query_label: int32 [2, 32, 384], P(None, ('dp', 'query')), may hold values 0 or 1
- query_live: int32 [16, 2, 2], P('dp', None, 'query'), may hold values from 1 to 384, 480 in all within a row
Outputs:
- block_out: bfloat16 [2, 32, 128, 1280], P(None, ('dp', 'query'))
- grad_tokens: float32 [2, 32, 128, 1280], P(None, ('dp', 'query'))
- grad_qkv: float32 [1280, 3840], P('dp')
- grad_out: float32 [1280, 1280], P('dp')
- grad_up: float32 [1280, 5120], P('dp')
- grad_down: float32 [5120, 1280], P('dp')
- grad_attn_gain: float32 [1280], P('dp')
- grad_ffn_gain: float32 [1280], P('dp')
- grad_up_bias: float32 [5120], P('dp')
- grad_cell: float32 [1280, 5120], P('dp')
- grad_gene: float32 [1280, 5120], P('dp')
- grad_decoder_bias: float32 [5120], P('dp')
- grad_readout: float32 [5120], P('dp')
Inputs may be any that keep to these rules, and one draw needn't show every extreme that they name: `query_live`: the 2 devices of one dp index together hold 480 live rows in each micro-batch; a device's live rows are its first slots. `query_cell`: index of a cell within the query group of the row's device.
All inputs are finite; a program needn't handle non-finite values. No bound on the sum of `query_label` on one device may be relied on, other than what follows from the above.
Results may differ from a plain program's by a relative error of at most 0.02.
Values may be sent and summed in bfloat16 or wider, within the bound.
No kernel may reach another device: no remote copies, remote signals or barrier semaphores. Data moves between devices by JAX's collectives and lax.ppermute only.
A program may use at most 320 MiB of HBM per device.

v0:
```python
import jax
import jax.numpy as jnp
from jax import lax
from jax.sharding import PartitionSpec as P

D = 1280
HEADS = 20
HEAD = 64
highest = lax.Precision.HIGHEST
epsilon = 1e-05


def row_product(left, right):
    return lax.dot_general(
        left, right, (((0,), (0,)), ((), ())), preferred_element_type=jnp.float32
    )


def times_transpose(left, right):
    return lax.dot_general(
        left, right, (((1,), (1,)), ((), ())), preferred_element_type=jnp.float32
    )


def layer_stats(values):
    average = jnp.mean(values, axis=-1, keepdims=True)
    centred = values - average
    variance = jnp.mean(centred * centred, axis=-1, keepdims=True)
    inverse = lax.rsqrt(variance + epsilon)
    return (centred * inverse, inverse)


def norm_back(grad_scaled, gain, normal, inverse):
    grad_normal = grad_scaled * gain
    along_normal = jnp.mean(grad_normal * normal, axis=-1, keepdims=True)
    average = jnp.mean(grad_normal, axis=-1, keepdims=True)
    grad_values = inverse * (grad_normal - average - normal * along_normal)
    return (grad_values, jnp.sum(grad_scaled * normal, axis=0))


def encode(inputs, weights):
    qkv_weight, out_weight, up_weight, down_weight, attn_gain, ffn_gain, up_bias = weights
    length = inputs.shape[0]
    tokens_wide = inputs.astype(jnp.float32)
    norm_one, scale_one = layer_stats(tokens_wide)
    normed = (norm_one * attn_gain.astype(jnp.float32)).astype(jnp.bfloat16)
    projected = jnp.dot(normed, qkv_weight, preferred_element_type=jnp.float32).astype(jnp.bfloat16)
    projected = projected.reshape(length, 3, HEADS, HEAD)
    queries = projected[:, 0]
    key_heads = projected[:, 1]
    value_heads = projected[:, 2]
    scores = (
        jnp.einsum("qhd,khd->hqk", queries, key_heads, preferred_element_type=jnp.float32) * 0.125
    )
    row_max = jnp.max(scores, axis=-1, keepdims=True)
    shifted = jnp.exp(scores - row_max)
    row_total = jnp.sum(shifted, axis=-1, keepdims=True)
    attn_probs = (shifted / row_total).astype(jnp.bfloat16)
    logsum = row_max + jnp.log(row_total)
    mixed_heads = jnp.einsum(
        "hqk,khd->qhd", attn_probs, value_heads, preferred_element_type=jnp.float32
    )
    mixed_heads = mixed_heads.astype(jnp.bfloat16).reshape(length, D)
    hidden = tokens_wide + jnp.dot(mixed_heads, out_weight, preferred_element_type=jnp.float32)
    norm_two, scale_two = layer_stats(hidden)
    second = (norm_two * ffn_gain.astype(jnp.float32)).astype(jnp.bfloat16)
    up_proj = jnp.dot(second, up_weight, preferred_element_type=jnp.float32) + up_bias.astype(
        jnp.float32
    )
    active = jax.nn.gelu(up_proj, approximate=True).astype(jnp.bfloat16)
    output = hidden + jnp.dot(active, down_weight, preferred_element_type=jnp.float32)
    saved_state = (
        norm_one,
        scale_one,
        normed,
        queries,
        key_heads,
        value_heads,
        logsum,
        mixed_heads,
        norm_two,
        scale_two,
        second,
        up_proj,
        active,
    )
    return (output, saved_state)


def encode_back(grad_output, saved_state, weights):
    qkv_weight, out_weight, up_weight, down_weight, attn_gain, ffn_gain = weights
    (
        norm_one,
        scale_one,
        normed,
        queries,
        key_heads,
        value_heads,
        logsum,
        mixed_heads,
        norm_two,
        scale_two,
        second,
        up_proj,
        active,
    ) = saved_state
    length = grad_output.shape[0]
    grad_branch = grad_output.astype(jnp.bfloat16)
    grad_down = row_product(active, grad_branch)
    grad_active = times_transpose(grad_branch, down_weight)
    gelu_back = jax.vjp(lambda inner_values: jax.nn.gelu(inner_values, approximate=True), up_proj)[
        1
    ]
    grad_up_proj = gelu_back(grad_active)[0].astype(jnp.bfloat16)
    grad_up = row_product(second, grad_up_proj)
    grad_up_bias = jnp.sum(grad_up_proj.astype(jnp.float32), axis=0)
    grad_second = times_transpose(grad_up_proj, up_weight)
    grad_hidden_norm, grad_ffn_gain = norm_back(
        grad_second, ffn_gain.astype(jnp.float32), norm_two, scale_two
    )
    grad_hidden = grad_output + grad_hidden_norm
    grad_attn = grad_hidden.astype(jnp.bfloat16)
    grad_out = row_product(mixed_heads, grad_attn)
    grad_mixed = (
        times_transpose(grad_attn, out_weight).astype(jnp.bfloat16).reshape(length, HEADS, HEAD)
    )
    scores = (
        jnp.einsum("qhd,khd->hqk", queries, key_heads, preferred_element_type=jnp.float32) * 0.125
    )
    attn_probs = jnp.exp(scores - logsum)
    probs_low = attn_probs.astype(jnp.bfloat16)
    grad_values = jnp.einsum(
        "hqk,qhd->khd", probs_low, grad_mixed, preferred_element_type=jnp.float32
    )
    grad_probs = jnp.einsum(
        "qhd,khd->hqk", grad_mixed, value_heads, preferred_element_type=jnp.float32
    )
    along_probs = jnp.sum(grad_probs * attn_probs, axis=-1, keepdims=True)
    grad_scores = (attn_probs * (grad_probs - along_probs) * 0.125).astype(jnp.bfloat16)
    grad_queries = jnp.einsum(
        "hqk,khd->qhd", grad_scores, key_heads, preferred_element_type=jnp.float32
    )
    grad_keys = jnp.einsum("hqk,qhd->khd", grad_scores, queries, preferred_element_type=jnp.float32)
    grad_projected = (
        jnp.stack([grad_queries, grad_keys, grad_values], axis=1)
        .astype(jnp.bfloat16)
        .reshape(length, 3 * D)
    )
    grad_qkv = row_product(normed, grad_projected)
    grad_normed = times_transpose(grad_projected, qkv_weight)
    grad_input_norm, grad_attn_gain = norm_back(
        grad_normed, attn_gain.astype(jnp.float32), norm_one, scale_one
    )
    grad_input = grad_hidden + grad_input_norm
    return (
        (grad_qkv, grad_out, grad_up, grad_down, grad_attn_gain, grad_ffn_gain, grad_up_bias),
        grad_input,
    )


def decode(summary_all, weights, gene_rows, cell_ids, labels, live_count):
    cell_weight, gene_weight, decoder_bias, readout = weights
    group_size = summary_all.shape[0]
    slot_count = gene_rows.shape[0]
    cell_part = jnp.dot(summary_all, cell_weight, preferred_element_type=jnp.float32)
    onehot = (cell_ids[:, None] == jnp.arange(group_size, dtype=jnp.int32)[None, :]).astype(
        jnp.float32
    )
    picked = jnp.dot(onehot, cell_part, precision=highest)
    pre_act = (
        picked
        + jnp.dot(gene_rows, gene_weight, preferred_element_type=jnp.float32)
        + decoder_bias.astype(jnp.float32)
    )
    activity, silu_back = jax.vjp(jax.nn.silu, pre_act)
    read_wide = readout.astype(jnp.float32)
    logits = jnp.sum(activity * read_wide[None, :], axis=-1)
    live_rows = (jnp.arange(slot_count, dtype=jnp.int32) < live_count).astype(jnp.float32)
    grad_logits = live_rows * (jax.nn.sigmoid(logits) - labels.astype(jnp.float32))
    grad_readout = jnp.sum(grad_logits[:, None] * activity, axis=0)
    grad_pre = silu_back(grad_logits[:, None] * read_wide[None, :])[0].astype(jnp.bfloat16)
    grad_pre_wide = grad_pre.astype(jnp.float32)
    grad_decoder_bias = jnp.sum(grad_pre_wide, axis=0)
    grad_gene = row_product(gene_rows, grad_pre)
    grad_cellproj = lax.dot_general(
        onehot, grad_pre_wide, (((0,), (0,)), ((), ())), precision=highest
    )
    grad_cell = lax.dot_general(
        summary_all.astype(jnp.float32), grad_cellproj, (((0,), (0,)), ((), ())), precision=highest
    )
    grad_summary = lax.dot_general(
        grad_cellproj, cell_weight.astype(jnp.float32), (((1,), (1,)), ((), ())), precision=highest
    )
    return ((grad_cell, grad_gene, grad_decoder_bias, grad_readout), grad_summary)


def shards(
    tokens,
    out_cotangent,
    qkv_weight,
    out_weight,
    up_weight,
    down_weight,
    attn_gain,
    ffn_gain,
    up_bias,
    cell_weight,
    gene_weight,
    decoder_bias,
    readout,
    gene_embed,
    query_cell,
    query_label,
    query_live,
):
    micro_count = tokens.shape[0]
    outputs = []
    input_grads = []
    totals = None
    for micro_index in range(micro_count):
        gathered = (
            lax.all_gather(qkv_weight, "dp", axis=0, tiled=True),
            lax.all_gather(out_weight, "dp", axis=0, tiled=True),
            lax.all_gather(up_weight, "dp", axis=0, tiled=True),
            lax.all_gather(down_weight, "dp", axis=0, tiled=True),
            lax.all_gather(attn_gain, "dp", axis=0, tiled=True),
            lax.all_gather(ffn_gain, "dp", axis=0, tiled=True),
            lax.all_gather(up_bias, "dp", axis=0, tiled=True),
            lax.all_gather(cell_weight, "dp", axis=0, tiled=True),
            lax.all_gather(gene_weight, "dp", axis=0, tiled=True),
            lax.all_gather(decoder_bias, "dp", axis=0, tiled=True),
            lax.all_gather(readout, "dp", axis=0, tiled=True),
        )
        output, saved_state = encode(tokens[micro_index, 0], gathered[:7])
        outputs.append(output.astype(jnp.bfloat16))
        summary_all = lax.all_gather(output[0:1].astype(jnp.bfloat16), "query", axis=0, tiled=True)
        decoder_grads, grad_summary = decode(
            summary_all,
            gathered[7:],
            gene_embed[micro_index, 0],
            query_cell[micro_index, 0],
            query_label[micro_index, 0],
            query_live[0, micro_index, 0],
        )
        grad_own = lax.psum_scatter(
            grad_summary.astype(jnp.bfloat16), "query", scatter_dimension=0, tiled=True
        ).astype(jnp.float32)
        grad_output = out_cotangent[micro_index, 0].astype(jnp.float32)
        grad_output = grad_output.at[0:1].add(grad_own)
        back_weights = (
            lax.all_gather(qkv_weight, "dp", axis=0, tiled=True),
            lax.all_gather(out_weight, "dp", axis=0, tiled=True),
            lax.all_gather(up_weight, "dp", axis=0, tiled=True),
            lax.all_gather(down_weight, "dp", axis=0, tiled=True),
            lax.all_gather(attn_gain, "dp", axis=0, tiled=True),
            lax.all_gather(ffn_gain, "dp", axis=0, tiled=True),
        )
        encoder_grads, grad_input = encode_back(grad_output, saved_state, back_weights)
        input_grads.append(grad_input)
        step_grads = encoder_grads + decoder_grads
        if micro_index == 0:
            totals = tuple(step_grads)
        else:
            totals = tuple((earlier + later for earlier, later in zip(totals, step_grads)))
    owned = (
        lax.psum_scatter(
            totals[0].astype(jnp.bfloat16), "dp", scatter_dimension=0, tiled=True
        ).astype(jnp.float32),
        lax.psum_scatter(
            totals[1].astype(jnp.bfloat16), "dp", scatter_dimension=0, tiled=True
        ).astype(jnp.float32),
        lax.psum_scatter(
            totals[2].astype(jnp.bfloat16), "dp", scatter_dimension=0, tiled=True
        ).astype(jnp.float32),
        lax.psum_scatter(
            totals[3].astype(jnp.bfloat16), "dp", scatter_dimension=0, tiled=True
        ).astype(jnp.float32),
        lax.psum_scatter(
            totals[4].astype(jnp.bfloat16), "dp", scatter_dimension=0, tiled=True
        ).astype(jnp.float32),
        lax.psum_scatter(
            totals[5].astype(jnp.bfloat16), "dp", scatter_dimension=0, tiled=True
        ).astype(jnp.float32),
        lax.psum_scatter(
            totals[6].astype(jnp.bfloat16), "dp", scatter_dimension=0, tiled=True
        ).astype(jnp.float32),
        lax.psum_scatter(
            totals[7].astype(jnp.bfloat16), "dp", scatter_dimension=0, tiled=True
        ).astype(jnp.float32),
        lax.psum_scatter(
            totals[8].astype(jnp.bfloat16), "dp", scatter_dimension=0, tiled=True
        ).astype(jnp.float32),
        lax.psum_scatter(
            totals[9].astype(jnp.bfloat16), "dp", scatter_dimension=0, tiled=True
        ).astype(jnp.float32),
        lax.psum_scatter(
            totals[10].astype(jnp.bfloat16), "dp", scatter_dimension=0, tiled=True
        ).astype(jnp.float32),
    )
    totals = (
        lax.psum(owned[0].astype(jnp.bfloat16), "query").astype(jnp.float32),
        lax.psum(owned[1].astype(jnp.bfloat16), "query").astype(jnp.float32),
        lax.psum(owned[2].astype(jnp.bfloat16), "query").astype(jnp.float32),
        lax.psum(owned[3].astype(jnp.bfloat16), "query").astype(jnp.float32),
        lax.psum(owned[4].astype(jnp.bfloat16), "query").astype(jnp.float32),
        lax.psum(owned[5].astype(jnp.bfloat16), "query").astype(jnp.float32),
        lax.psum(owned[6].astype(jnp.bfloat16), "query").astype(jnp.float32),
        lax.psum(owned[7].astype(jnp.bfloat16), "query").astype(jnp.float32),
        lax.psum(owned[8].astype(jnp.bfloat16), "query").astype(jnp.float32),
        lax.psum(owned[9].astype(jnp.bfloat16), "query").astype(jnp.float32),
        lax.psum(owned[10].astype(jnp.bfloat16), "query").astype(jnp.float32),
    )
    block_out = jnp.stack(outputs, axis=0)[:, None]
    grad_tokens = jnp.stack(input_grads, axis=0)[:, None]
    return (
        block_out,
        grad_tokens,
        totals[0],
        totals[1],
        totals[2],
        totals[3],
        totals[4],
        totals[5],
        totals[6],
        totals[7],
        totals[8],
        totals[9],
        totals[10],
    )


def solution(mesh):
    placed = (
        P(None, ("dp", "query"), None, None),
        P(None, ("dp", "query"), None, None),
        P("dp", None),
        P("dp", None),
        P("dp", None),
        P("dp", None),
        P("dp"),
        P("dp"),
        P("dp"),
        P("dp", None),
        P("dp", None),
        P("dp"),
        P("dp"),
        P(None, ("dp", "query"), None, None),
        P(None, ("dp", "query"), None),
        P(None, ("dp", "query"), None),
        P("dp", None, "query"),
    )
    return jax.shard_map(
        shards,
        mesh=mesh,
        in_specs=placed,
        out_specs=(
            P(None, ("dp", "query"), None, None),
            P(None, ("dp", "query"), None, None),
            P("dp", None),
            P("dp", None),
            P("dp", None),
            P("dp", None),
            P("dp"),
            P("dp"),
            P("dp"),
            P("dp", None),
            P("dp", None),
            P("dp"),
            P("dp"),
        ),
        check_vma=False,
    )
```

profile of v0, /device:TPU:0, one launch (start us, length us, event | category | flops | bytes accessed | tf_op | source)
XLA Modules:
  0.0 1549.0 jit_solution(1948422574728645002)
XLA Ops:
  14.5 65.3 %all-reduce.13 = (bf16[1280]{0:T(1024)(128)(2,1)S(1)}, bf16[5120]{0:T(1024)(128)(2,1)S(1)}, bf16[1280]{0:T(1024)(128)(2,1)S(1)}, bf16[5120]{0:T(1024)(128)(2,1)S(1)}, bf16[5120]{0:T(1024)(128)(2,1)S(1)}) all-reduce(bf16[1280]{0:T(1024)(128)(2,1)S(1)} %dynamic-update-slice.6, ...), channel_id=1, replica_groups=mesh['dp'=16,'query'=2] {'dp'}, use_global_device_ids=true, to_apply=%add | all-reduce | flops 17920 | bytes 71680
  81.0 16.6 %all-gather.9.cloned.1.call-done = bf16[1280,3840]{1,0:T(8,128)(2,1)} async-done(((bf16[80,3840]{1,0:T(8,128)(2,1)}), bf16[1280,3840]{1,0:T(8,128)(2,1)}) %all-gather.9.cloned.1.call-update) | async-done | bytes 9830416 | tf_op jit(solution)/shard_map/all_gather | solution.py:222
  112.9 31.2 %all-gather.11.cloned.1.call-done = bf16[1280,1280]{1,0:T(8,128)(2,1)} async-done(((bf16[80,1280]{1,0:T(8,128)(2,1)}), bf16[1280,1280]{1,0:T(8,128)(2,1)}) %all-gather.11.cloned.1.call-update) | async-done | bytes 3276816 | tf_op jit(solution)/shard_map/all_gather | solution.py:223
  151.0 98.3 %all-gather.13.cloned.1.call-done = bf16[1280,5120]{1,0:T(8,128)(2,1)} async-done(((bf16[80,5120]{1,0:T(8,128)(2,1)}), bf16[1280,5120]{1,0:T(8,128)(2,1)}) %all-gather.13.cloned.1.call-update) | async-done | bytes 13107216 | tf_op jit(solution)/shard_map/all_gather | solution.py:224
  257.5 96.1 %all-gather.15.cloned.1.call-done = bf16[5120,1280]{1,0:T(8,128)(2,1)} async-done(((bf16[320,1280]{1,0:T(8,128)(2,1)}), bf16[5120,1280]{1,0:T(8,128)(2,1)}) %all-gather.15.cloned.1.call-update) | async-done | bytes 13107216 | tf_op jit(solution)/shard_map/all_gather | solution.py:225
  375.1 82.8 %all-gather.17.cloned.1.call-done = bf16[1280,5120]{1,0:T(8,128)(2,1)} async-done(((bf16[80,5120]{1,0:T(8,128)(2,1)}), bf16[1280,5120]{1,0:T(8,128)(2,1)}) %all-gather.17.cloned.1.call-update) | async-done | bytes 13107216 | tf_op jit(solution)/shard_map/all_gather | solution.py:229
  464.5 97.8 %all-gather.19.cloned.1.call-done = bf16[1280,5120]{1,0:T(8,128)(2,1)} async-done(((bf16[80,5120]{1,0:T(8,128)(2,1)}), bf16[1280,5120]{1,0:T(8,128)(2,1)}) %all-gather.19.cloned.1.call-update) | async-done | bytes 13107216 | tf_op jit(solution)/shard_map/all_gather | solution.py:230
  615.9 12.7 fusion.51
  628.6 16.2 %fusion.2 = bf16[1280,5120]{0,1:T(8,128)(2,1)} fusion(f32[5120,1280]{1,0:T(8,128)} %fusion.51, bf16[384,5120]{1,0:T(8,128)(2,1)} %get-tuple-element.137, bf16[2,1,384,1280]{3,2,1,0:T(8,128)(2,1)} %param.34), kind=kOutput, calls=%fused_computation.7 | convolution fusion | flops 5046272000 | bytes 44236800 | tf_op jit(solution)/shard_map/dot_general | solution.py:14
  644.8 17.6 %copy.89 = bf16[1280,5120]{1,0:T(8,128)(2,1)} copy(bf16[1280,5120]{0,1:T(8,128)(2,1)} %fusion.2) | data formatting | bytes 26214400
  670.4 14.2 convolution_convert_fusion.5
  684.5 13.5 convolution_convert_fusion.4
  806.7 12.7 fusion.185
  819.5 15.7 %add_convert_fusion.3 = bf16[1280,5120]{1,0:T(8,128)(2,1)} fusion(f32[1280,5120]{1,0:T(8,128)} %fusion.185, bf16[128,5120]{1,0:T(8,128)(2,1)} %copy-done.26, f32[128,1280]{1,0:T(8,128)S(1)} %copy-done.6, f32[128]{0:T(128)S(1)} %copy-done.75, f32[128]{0:T(128)S(1)} %copy-done.70, f32[1280]{0:T(1024)S(1)} %convert_element_type.331), kind=kOutput, calls=%fused_computation.5 | convolution fusion | flops 1691484160 | bytes 41293824 | tf_op jit(solution)/shard_map/dot_general | solution.py:14
  836.3 12.8 fusion.146
  849.1 16.3 %add_convert_fusion.2 = bf16[5120,1280]{1,0:T(8,128)(2,1)} fusion(f32[5120,1280]{1,0:T(8,128)} %fusion.146, f32[128,1280]{1,0:T(8,128)S(1)} %copy-done.22, f32[128,5120]{1,0:T(8,128)} %convolution_add_fusion.1), kind=kOutput, calls=%fused_computation.4 | convolution fusion | flops 1696890880 | bytes 42598400 | tf_op jit(solution)/shard_map/dot_general | solution.py:14
  866.1 13.9 fusion.167
  880.0 19.8 %add_convert_fusion.1 = bf16[1280,5120]{1,0:T(8,128)(2,1)} fusion(f32[1280,5120]{1,0:T(8,128)} %fusion.167, f32[2,5120]{1,0:T(2,128)S(1)} %fusion.134, bf16[2,1,1280]{2,1,0:T(2,128)(2,1)S(1)} %copy-done.61), kind=kOutput, calls=%fused_computation.3 | convolution fusion | flops 170393600 | bytes 39367680 | tf_op jit(solution)/shard_map/dot_general | solution.py:188
  903.5 83.3 %reduce-scatter.9.cloned.1.call-done = bf16[80,3840]{1,0:T(8,128)(2,1)} async-done(((bf16[1280,3840]{1,0:T(8,128)(2,1)}), bf16[80,3840]{1,0:T(8,128)(2,1)}) %reduce-scatter.9.cloned.1.call-update) | async-done | bytes 614416 | tf_op jit(solution)/shard_map/reduce_scatter | solution.py:266
  986.8 142.1 %reduce-scatter.13.cloned.1.call-done = bf16[80,5120]{1,0:T(8,128)(2,1)} async-done(((bf16[1280,5120]{1,0:T(8,128)(2,1)}), bf16[80,5120]{1,0:T(8,128)(2,1)}) %reduce-scatter.13.cloned.1.call-update) | async-done | bytes 819216 | tf_op jit(solution)/shard_map/reduce_scatter | solution.py:272
  1128.9 142.2 %reduce-scatter.15.cloned.1.call-done = bf16[320,1280]{1,0:T(8,128)(2,1)} async-done(((bf16[5120,1280]{1,0:T(8,128)(2,1)}), bf16[320,1280]{1,0:T(8,128)(2,1)}) %reduce-scatter.15.cloned.1.call-update) | async-done | bytes 819216 | tf_op jit(solution)/shard_map/reduce_scatter | solution.py:275
  1271.1 141.5 %reduce-scatter.17.cloned.1.call-done = bf16[80,5120]{1,0:T(8,128)(2,1)} async-done(((bf16[1280,5120]{1,0:T(8,128)(2,1)}), bf16[80,5120]{1,0:T(8,128)(2,1)}) %reduce-scatter.17.cloned.1.call-update) | async-done | bytes 819216 | tf_op jit(solution)/shard_map/reduce_scatter | solution.py:287
  1428.5 59.6 %all-reduce.12 = (bf16[1280]{0:T(1024)(128)(2,1)S(1)}, bf16[1280]{0:T(1024)(128)(2,1)S(1)}, bf16[5120]{0:T(1024)(128)(2,1)S(1)}, bf16[5120]{0:T(1024)(128)(2,1)S(1)}, bf16[5120]{0:T(1024)(128)(2,1)S(1)}) all-reduce(bf16[1280]{0:T(1024)(128)(2,1)S(1)} %add_convert_fusion.9, ...), channel_id=8, replica_groups=mesh['dp'=16,'query'=2] {'dp'}, use_global_device_ids=true, to_apply=%region_36.37.clone | all-reduce | flops 17920 | bytes 71680
  1499.9 33.9 %all-reduce.19.cloned.1.call-done = (bf16[80,5120]{0,1:T(8,128)(2,1)}, bf16[80,3840]{1,0:T(8,128)(2,1)}, bf16[80,1280]{1,0:T(8,128)(2,1)}, bf16[80,5120]{1,0:T(8...) async-done(((bf16[80,5120]{0,1:T(8,128)(2,1)}, bf16[80,3840]{1,0:T(8,128)(2,1)}, bf16[80,1280]{1,0:T(8,128)(2,1)}, bf16[80,5120]{1,0:T(8,128)(2,1)}, ...) | async-done | bytes 4096016 | tf_op jit(solution)/shard_map/psum | solution.py:309
  (359 shorter events, 275.0 us)
Async XLA Ops:
  7.3 90.3 %all-gather.9.cloned.1.call-start = ((), (), s32[]{:S(2)}) async-start(), calls=%async_computation.6 | async-start | bytes 10444800 | tf_op jit(solution)/shard_map/all_gather | solution.py:222
  8.0 136.1 %all-gather.11.cloned.1.call-start = ((), (), s32[]{:S(2)}) async-start(), calls=%async_computation.7 | async-start | bytes 3481600 | tf_op jit(solution)/shard_map/all_gather | solution.py:223
  8.8 240.5 %all-gather.13.cloned.1.call-start = ((), (), s32[]{:S(2)}) async-start(), calls=%async_computation.8 | async-start | bytes 13926400 | tf_op jit(solution)/shard_map/all_gather | solution.py:224
  9.5 344.1 %all-gather.15.cloned.1.call-start = ((), (), s32[]{:S(2)}) async-start(), calls=%async_computation.9 | async-start | bytes 13926400 | tf_op jit(solution)/shard_map/all_gather | solution.py:225
  10.1 447.9 %all-gather.17.cloned.1.call-start = ((), (), s32[]{:S(2)}) async-start(), calls=%async_computation.10 | async-start | bytes 13926400 | tf_op jit(solution)/shard_map/all_gather | solution.py:229
  10.7 551.6 %all-gather.19.cloned.1.call-start = ((), (), s32[]{:S(2)}) async-start(), calls=%async_computation.11 | async-start | bytes 13926400 | tf_op jit(solution)/shard_map/all_gather | solution.py:230
  11.2 889.9 %reduce-scatter.19.cloned.1.call-start = ((), (), s32[]{:S(2)}) async-start(), calls=%async_computation.17 | async-start | bytes 13926400
  146.8 605.1 %copy-start.5 = (f32[128,1280]{1,0:T(8,128)}, f32[128,1280]{1,0:T(8,128)S(1)}, u32[]{:S(2)}) copy-start(f32[128,1280]{1,0:T(8,128)S(1)} %get-tuple-element.146) | copy-start | bytes 1966084
  146.8 102.5 %copy-start.69 = (f32[128]{0:T(128)}, f32[128]{0:T(128)S(1)}, u32[]{:S(2)}) copy-start(f32[128]{0:T(128)S(1)} %broadcast_multiply_fusion.8) | copy-start | bytes 1540
  150.7 589.7 %copy-start.9 = (f32[128,1280]{1,0:T(8,128)}, f32[128,1280]{1,0:T(8,128)S(1)}, u32[]{:S(2)}) copy-start(f32[128,1280]{1,0:T(8,128)S(1)} %get-tuple-element.150) | copy-start | bytes 1966084
  151.0 106.5 %copy-start.74 = (f32[128]{0:T(128)}, f32[128]{0:T(128)S(1)}, u32[]{:S(2)}) copy-start(f32[128]{0:T(128)S(1)} %add_rsqrt_fusion) | copy-start | bytes 1540
  366.3 91.6 %copy-start.60 = (bf16[2,1,1280]{2,1,0:T(2,128)(2,1)}, bf16[2,1,1280]{2,1,0:T(2,128)(2,1)S(1)}, u32[]{:S(2)}) copy-start(bf16[2,1,1280]{2,1,0:T(2,128)(2,1)S(1)} %all-gather.1) | copy-start | bytes 15364
  370.8 93.7 %copy-start.47 = (bf16[128,1280]{1,0:T(8,128)(2,1)}, bf16[128,1280]{1,0:T(8,128)(2,1)S(1)}, u32[]{:S(2)}) copy-start(bf16[128,1280]{1,0:T(8,128)(2,1)S(1)} %fusion.26) | copy-start | bytes 983044
  375.1 216.6 %copy-start.62 = (bf16[2,1,1280]{2,1,0:T(2,128)(2,1)}, bf16[2,1,1280]{2,1,0:T(2,128)(2,1)S(1)}, u32[]{:S(2)}) copy-start(bf16[2,1,1280]{2,1,0:T(2,128)(2,1)S(1)} %all-gather) | copy-start | bytes 15364
  662.5 241.1 %reduce-scatter.11.cloned.1.call-start = ((), (), s32[]{:S(2)}) async-start(), calls=%async_computation.13 | async-start | bytes 3481600 | tf_op jit(solution)/shard_map/reduce_scatter | solution.py:269
  755.8 231.0 %reduce-scatter.9.cloned.1.call-start = ((), (), s32[]{:S(2)}) async-start(), calls=%async_computation.12 | async-start | bytes 10444800 | tf_op jit(solution)/shard_map/reduce_scatter | solution.py:266
  805.7 323.3 %reduce-scatter.13.cloned.1.call-start = ((), (), s32[]{:S(2)}) async-start(), calls=%async_computation.14 | async-start | bytes 13926400 | tf_op jit(solution)/shard_map/reduce_scatter | solution.py:272
  835.2 435.9 %reduce-scatter.15.cloned.1.call-start = ((), (), s32[]{:S(2)}) async-start(), calls=%async_computation.15 | async-start | bytes 13926400 | tf_op jit(solution)/shard_map/reduce_scatter | solution.py:275
  865.4 547.1 %reduce-scatter.17.cloned.1.call-start = ((), (), s32[]{:S(2)}) async-start(), calls=%async_computation.16 | async-start | bytes 13926400 | tf_op jit(solution)/shard_map/reduce_scatter | solution.py:287
  899.8 633.9 %all-reduce.19.cloned.1.call-start = ((), (), s32[]{:S(2)}) async-start(), calls=%async_computation.18 | async-start | bytes 9175040 | tf_op jit(solution)/shard_map/psum | solution.py:309
  1419.9 76.4 %copy-start.46 = (bf16[128,1280]{1,0:T(8,128)(2,1)S(1)}, bf16[128,1280]{1,0:T(8,128)(2,1)}, u32[]{:S(2)}) copy-start(bf16[128,1280]{1,0:T(8,128)(2,1)} %copy-done.45) | copy-start | bytes 983044
  1419.9 76.4 %copy-start.48 = (bf16[128,1280]{1,0:T(8,128)(2,1)S(1)}, bf16[128,1280]{1,0:T(8,128)(2,1)}, u32[]{:S(2)}) copy-start(bf16[128,1280]{1,0:T(8,128)(2,1)} %copy-done.47) | copy-start | bytes 983044
  1419.9 77.3 %copy-start.18 = (f32[128,1280]{1,0:T(8,128)S(1)}, f32[128,1280]{1,0:T(8,128)}, u32[]{:S(2)}) copy-start(f32[128,1280]{1,0:T(8,128)} %copy-done.17) | copy-start | bytes 1966084
  1419.9 77.2 %copy-start.20 = (f32[128,1280]{1,0:T(8,128)S(1)}, f32[128,1280]{1,0:T(8,128)}, u32[]{:S(2)}) copy-start(f32[128,1280]{1,0:T(8,128)} %copy-done.19) | copy-start | bytes 1966084
  (89 other events, 984.1 us)
Sparse Core Ops, SparseCore 0:
  10.4 87.1 all-gather.8
  99.9 44.1 all-gather.10
  146.4 102.8 all-gather.12
  251.4 102.1 all-gather.14
  355.7 102.1 all-gather.16
  460.1 102.1 all-gather.18
  662.6 136.5 reduce-scatter.18
  803.4 65.9 reduce-scatter.10
  873.6 113.2 reduce-scatter.8
  990.8 138.1 reduce-scatter.12
  1133.6 137.4 reduce-scatter.14
  1275.1 137.4 reduce-scatter.16
  1416.4 117.3 all-reduce.18
where the time goes:
time: 1560 us; the launch traced here: 1550 us
  waiting for transfers between devices  969 us (62%)
  matrix products  339 us (22%)
  blocking collectives  147 us (9%)
  local copies, waits for them, and re-layouts  41 us (3%)
  other arithmetic  33.2 us (2%)
  between operations  18 us (1%)
    reduce_scatter x1, waiting for transfers between devices, shards(): lax.psum_scatter(totals[3].astype(jnp.bfloat16), 'dp', scatter_dimension=...  142 us
    reduce_scatter x1, waiting for transfers between devices, shards(): lax.psum_scatter(totals[2].astype(jnp.bfloat16), 'dp', scatter_dimension=...  142 us
    reduce_scatter x1, waiting for transfers between devices, shards(): lax.psum_scatter(totals[7].astype(jnp.bfloat16), 'dp', scatter_dimension=...  141 us
    unnamed x3, blocking collectives  133 us
    dot_general x10, matrix products, row_product(): lax.dot_general(left, right, (((0,), (0,)), ((), ())), preferred_element_...  110 us
    all_gather x1, waiting for transfers between devices, shards(): lax.all_gather(up_weight, 'dp', axis=0, tiled=True)  98.3 us
    all_gather x1, waiting for transfers between devices, shards(): lax.all_gather(gene_weight, 'dp', axis=0, tiled=True)  97.8 us
    all_gather x1, waiting for transfers between devices, shards(): lax.all_gather(down_weight, 'dp', axis=0, tiled=True)  96.1 us
  transfers between devices with their start and end apart: 13, of which 11 were waited for; matrix products, arithmetic and copies ran while one was open for 19% of the time, Pallas kernels for 0%

commit v1 on v0

--- a/solution.py
+++ b/solution.py
@@ -8,6 +8,18 @@
 HEAD = 64
 highest = lax.Precision.HIGHEST
 epsilon = 1e-05
+
+
+def collect(x, axis, dim):
+    ways, here = (lax.axis_size(axis), lax.axis_index(axis))
+    grown, reach = (x, 1)
+    while reach < ways:
+        theirs = lax.ppermute(grown, axis, [(d, d ^ reach) for d in range(ways)])
+        mine_first = jnp.concatenate([grown, theirs], axis=dim)
+        theirs_first = jnp.concatenate([theirs, grown], axis=dim)
+        grown = jnp.where(here & reach == 0, mine_first, theirs_first)
+        reach = 2 * reach
+    return grown
 
 
 def row_product(left, right):
@@ -227,7 +239,7 @@
             lax.all_gather(ffn_gain, "dp", axis=0, tiled=True),
             lax.all_gather(up_bias, "dp", axis=0, tiled=True),
             lax.all_gather(cell_weight, "dp", axis=0, tiled=True),
-            lax.all_gather(gene_weight, "dp", axis=0, tiled=True),
+            collect(gene_weight, "dp", 0),
             lax.all_gather(decoder_bias, "dp", axis=0, tiled=True),
             lax.all_gather(readout, "dp", axis=0, tiled=True),
         )

time: 1560 us -> 1730 us (1.11)
  blocking collectives: 147 us -> 246 us
  waiting for transfers between devices: 969 us -> 1020 us
    unnamed x3, blocking collectives: 133 us -> 232 us
    all_gather x1 -> x0, waiting for transfers between devices: 97.8 us -> none  [shards(): lax.all_gather(gene_weight, 'dp', axis=0, tiled=True)]
    all_gather x1, waiting for transfers between devices: 98.3 us -> 173 us  [shards(): lax.all_gather(up_weight, 'dp', axis=0, tiled=True)]
    ppermute x0 -> x4, waiting for transfers between devices: none -> 51.6 us  [collect(): theirs = lax.ppermute(grown, axis, [(d, d ^ reach) for d in range(ways)])]
    all_gather x1, waiting for transfers between devices: 96.1 us -> 135 us  [shards(): lax.all_gather(down_weight, 'dp', axis=0, tiled=True)]
    all_gather x1, waiting for transfers between devices: 82.8 us -> 116 us  [shards(): lax.all_gather(cell_weight, 'dp', axis=0, tiled=True)]
    all_gather x1, waiting for transfers between devices: 31.2 us -> 0.01 us  [shards(): lax.all_gather(out_weight, 'dp', axis=0, tiled=True)]
    unnamed x222 -> x246, local copies, waits for them, and re-layouts: 34.9 us -> 34.7 us
  transfers between devices with their start and end apart: 13 -> 16, of which waited for: 11 -> 10; matrix products, arithmetic and copies ran while one was open for 19% -> 19% of each run, Pallas kernels for 0% -> 0%
where the time goes in v1:
time: 1730 us
  waiting for transfers between devices  1020 us (59%)
  matrix products  343 us (20%)
  blocking collectives  246 us (14%)
  other arithmetic  48.1 us (3%)
  local copies, waits for them, and re-layouts  42.5 us (2%)
  between operations  18.7 us (1%)
    unnamed x3, blocking collectives  232 us
    all_gather x1, waiting for transfers between devices, shards(): lax.all_gather(up_weight, 'dp', axis=0, tiled=True)  173 us
    reduce_scatter x1, waiting for transfers between devices, shards(): lax.psum_scatter(totals[2].astype(jnp.bfloat16), 'dp', scatter_dimension=...  142 us
    reduce_scatter x1, waiting for transfers between devices, shards(): lax.psum_scatter(totals[3].astype(jnp.bfloat16), 'dp', scatter_dimension=...  142 us
    reduce_scatter x1, waiting for transfers between devices, shards(): lax.psum_scatter(totals[7].astype(jnp.bfloat16), 'dp', scatter_dimension=...  142 us
    all_gather x1, waiting for transfers between devices, shards(): lax.all_gather(down_weight, 'dp', axis=0, tiled=True)  135 us
    all_gather x1, waiting for transfers between devices, shards(): lax.all_gather(cell_weight, 'dp', axis=0, tiled=True)  116 us
    dot_general x10, matrix products, row_product(): lax.dot_general(left, right, (((0,), (0,)), ((), ())), preferred_element_...  110 us
  transfers between devices with their start and end apart: 16, of which 10 were waited for; matrix products, arithmetic and copies ran while one was open for 19% of the time, Pallas kernels for 0%

profile of v1, /device:TPU:0, one launch (start us, length us, event | category | flops | bytes accessed | tf_op | source)
XLA Modules:
  0.0 1725.6 jit_solution(849760421617607336)
XLA Ops:
  18.0 49.5 %collective-permute-done.1 = bf16[160,5120]{1,0:T(8,128)(2,1)} collective-permute-done((bf16[160,5120]{1,0:T(8,128)(2,1)S(1)}, bf16[160,5120]{1,0:T(8,128)(2,1)}, u32[]{:S(2)}, u32[]{:S(2)}) %collective-permute-start.1) | collective-permute-done | bytes 1638432 | tf_op jit(solution)/shard_map/ppermute | solution.py:17
  75.9 163.8 %all-reduce.13 = (bf16[1280]{0:T(1024)(128)(2,1)S(1)}, bf16[5120]{0:T(1024)(128)(2,1)S(1)}, bf16[1280]{0:T(1024)(128)(2,1)S(1)}, bf16[5120]{0:T(1024)(128)(2,1)S(1)}, bf16[5120]{0:T(1024)(128)(2,1)S(1)}) all-reduce(bf16[1280]{0:T(1024)(128)(2,1)S(1)} %dynamic-update-slice.6, ...), channel_id=1, replica_groups=mesh['dp'=16,'query'=2] {'dp'}, use_global_device_ids=true, to_apply=%add | all-reduce | flops 17920 | bytes 71680
  271.7 172.6 %all-gather.12.cloned.1.call-done = bf16[1280,5120]{1,0:T(8,128)(2,1)} async-done(((bf16[80,5120]{1,0:T(8,128)(2,1)}), bf16[1280,5120]{1,0:T(8,128)(2,1)}) %all-gather.12.cloned.1.call-update) | async-done | bytes 13107216 | tf_op jit(solution)/shard_map/all_gather | solution.py:236
  452.5 135.4 %all-gather.14.cloned.1.call-done = bf16[5120,1280]{1,0:T(8,128)(2,1)} async-done(((bf16[320,1280]{1,0:T(8,128)(2,1)}), bf16[5120,1280]{1,0:T(8,128)(2,1)}) %all-gather.14.cloned.1.call-update) | async-done | bytes 13107216 | tf_op jit(solution)/shard_map/all_gather | solution.py:237
  609.7 116.3 %all-gather.16.cloned.1.call-done = bf16[1280,5120]{1,0:T(8,128)(2,1)} async-done(((bf16[80,5120]{1,0:T(8,128)(2,1)}), bf16[1280,5120]{1,0:T(8,128)(2,1)}) %all-gather.16.cloned.1.call-update) | async-done | bytes 13107216 | tf_op jit(solution)/shard_map/all_gather | solution.py:241
  743.3 16.1 fusion.9
  759.3 17.9 %multiply_reduce_fusion.3 = (f32[384]{0:T(512)S(1)}, f32[384]{0:T(512)S(1)}, f32[384,5120]{1,0:T(8,128)}) fusion(f32[5120]{0:T(1024)S(1)} %convert_element_type.349, f32[384,5120]{1,0:T(8,128)} %fusion.9, f32[5120]{0:T(1024)S(1)} %convert_element_type.348, f32[384,5120]{1,0:T(8,128)S(1)} %fusion.137, bf16[640,5120]{1,0:T(8,128)(2,1)} %collective-permute-done.3, ...), kind=kOutput, calls=%fused_computation.33 | convolution fusion | flops 5119671296 | bytes 37727232 | tf_op jit(solution)/shard_map/dot_general | solution.py:184
  778.6 12.4 convert_reduce_fusion.1
  803.3 16.7 fusion.2
  820.0 17.6 %copy.89 = bf16[1280,5120]{1,0:T(8,128)(2,1)} copy(bf16[1280,5120]{0,1:T(8,128)(2,1)} %fusion.2) | data formatting | bytes 26214400
  844.8 14.2 convolution_convert_fusion.5
  859.0 14.0 convolution_convert_fusion.4
  983.3 12.8 fusion.189
  996.0 15.6 add_convert_fusion.3
  1012.8 12.7 fusion.148
  1025.5 16.3 add_convert_fusion.2
  1042.4 13.9 fusion.169
  1056.3 19.7 %add_convert_fusion.1 = bf16[1280,5120]{1,0:T(8,128)(2,1)} fusion(f32[1280,5120]{1,0:T(8,128)} %fusion.169, f32[2,5120]{1,0:T(2,128)S(1)} %fusion.134, bf16[2,1,1280]{2,1,0:T(2,128)(2,1)S(1)} %copy-done.69), kind=kOutput, calls=%fused_computation.3 | convolution fusion | flops 170393600 | bytes 39367680 | tf_op jit(solution)/shard_map/dot_general | solution.py:200
  1079.8 83.0 %reduce-scatter.9.cloned.1.call-done = bf16[80,3840]{1,0:T(8,128)(2,1)} async-done(((bf16[1280,3840]{1,0:T(8,128)(2,1)}), bf16[80,3840]{1,0:T(8,128)(2,1)}) %reduce-scatter.9.cloned.1.call-update) | async-done | bytes 614416 | tf_op jit(solution)/shard_map/reduce_scatter | solution.py:278
  1162.8 142.3 %reduce-scatter.13.cloned.1.call-done = bf16[80,5120]{1,0:T(8,128)(2,1)} async-done(((bf16[1280,5120]{1,0:T(8,128)(2,1)}), bf16[80,5120]{1,0:T(8,128)(2,1)}) %reduce-scatter.13.cloned.1.call-update) | async-done | bytes 819216 | tf_op jit(solution)/shard_map/reduce_scatter | solution.py:284
  1305.1 142.0 %reduce-scatter.15.cloned.1.call-done = bf16[320,1280]{1,0:T(8,128)(2,1)} async-done(((bf16[5120,1280]{1,0:T(8,128)(2,1)}), bf16[320,1280]{1,0:T(8,128)(2,1)}) %reduce-scatter.15.cloned.1.call-update) | async-done | bytes 819216 | tf_op jit(solution)/shard_map/reduce_scatter | solution.py:287
  1447.2 141.6 %reduce-scatter.17.cloned.1.call-done = bf16[80,5120]{1,0:T(8,128)(2,1)} async-done(((bf16[1280,5120]{1,0:T(8,128)(2,1)}), bf16[80,5120]{1,0:T(8,128)(2,1)}) %reduce-scatter.17.cloned.1.call-update) | async-done | bytes 819216 | tf_op jit(solution)/shard_map/reduce_scatter | solution.py:299
  1604.6 59.7 %all-reduce.12 = (bf16[1280]{0:T(1024)(128)(2,1)S(1)}, bf16[1280]{0:T(1024)(128)(2,1)S(1)}, bf16[5120]{0:T(1024)(128)(2,1)S(1)}, bf16[5120]{0:T(1024)(128)(2,1)S(1)}, bf16[5120]{0:T(1024)(128)(2,1)S(1)}) all-reduce(bf16[1280]{0:T(1024)(128)(2,1)S(1)} %add_convert_fusion.9, ...), channel_id=8, replica_groups=mesh['dp'=16,'query'=2] {'dp'}, use_global_device_ids=true, to_apply=%region_36.37.clone | all-reduce | flops 17920 | bytes 71680
  1676.1 33.7 %all-reduce.19.cloned.1.call-done = (bf16[80,5120]{0,1:T(8,128)(2,1)}, bf16[80,3840]{1,0:T(8,128)(2,1)}, bf16[80,1280]{1,0:T(8,128)(2,1)}, bf16[80,5120]{1,0:T(8...) async-done(((bf16[80,5120]{0,1:T(8,128)(2,1)}, bf16[80,3840]{1,0:T(8,128)(2,1)}, bf16[80,1280]{1,0:T(8,128)(2,1)}, bf16[80,5120]{1,0:T(8,128)(2,1)}, ...) | async-done | bytes 4096016 | tf_op jit(solution)/shard_map/psum | solution.py:321
  (391 shorter events, 267.1 us)
Async XLA Ops:
  7.2 242.0 %all-gather.8.cloned.1.call-start = ((), (), s32[]{:S(2)}) async-start(), calls=%async_computation.6 | async-start | bytes 10444800 | tf_op jit(solution)/shard_map/all_gather | solution.py:234
  7.9 256.7 %all-gather.10.cloned.1.call-start = ((), (), s32[]{:S(2)}) async-start(), calls=%async_computation.7 | async-start | bytes 3481600 | tf_op jit(solution)/shard_map/all_gather | solution.py:235
  8.7 435.6 %all-gather.12.cloned.1.call-start = ((), (), s32[]{:S(2)}) async-start(), calls=%async_computation.8 | async-start | bytes 13926400 | tf_op jit(solution)/shard_map/all_gather | solution.py:236
  9.4 578.5 %all-gather.14.cloned.1.call-start = ((), (), s32[]{:S(2)}) async-start(), calls=%async_computation.9 | async-start | bytes 13926400 | tf_op jit(solution)/shard_map/all_gather | solution.py:237
  10.0 716.0 %all-gather.16.cloned.1.call-start = ((), (), s32[]{:S(2)}) async-start(), calls=%async_computation.10 | async-start | bytes 13926400 | tf_op jit(solution)/shard_map/all_gather | solution.py:241
  10.6 1066.9 %reduce-scatter.19.cloned.1.call-start = ((), (), s32[]{:S(2)}) async-start(), calls=%async_computation.16 | async-start | bytes 13926400
  10.6 2.6 collective-permute-start
  15.0 52.5 %collective-permute-start.1 = (bf16[160,5120]{1,0:T(8,128)(2,1)S(1)}, bf16[160,5120]{1,0:T(8,128)(2,1)}, u32[]{:S(2)}, u32[]{:S(2)}) collective-permute-start(bf16[160,5120]{1,0:T(8,128)(2,1)S(1)} %maximum_select_fusion.5), channel_id=1, source_target_pairs={{0,4},{2,6},{4,0},{6,2},{8,12},{10,14},{12,8},{14,10},{16,20},{18,... | collective-permute-start | bytes 4915208 | tf_op jit(solution)/shard_map/ppermute | solution.py:17
  18.0 222.3 %copy-start.94 = (s32[2,1,384]{2,1,0:T(1,128)S(1)}, s32[2,1,384]{2,1,0:T(1,128)}, u32[]{:S(2)}) copy-start(s32[2,1,384]{2,1,0:T(1,128)} %param.35) | copy-start | bytes 9220
  18.0 222.3 %copy-start.95 = (s32[2,1,384]{2,1,0:T(1,128)S(1)}, s32[2,1,384]{2,1,0:T(1,128)}, u32[]{:S(2)}) copy-start(s32[2,1,384]{2,1,0:T(1,128)} %param.36) | copy-start | bytes 9220
  18.0 222.4 %copy-start.8 = (bf16[2,1,128,1280]{3,2,1,0:T(8,128)(2,1)S(1)}, bf16[2,1,128,1280]{3,2,1,0:T(8,128)(2,1)}, u32[]{:S(2)}) copy-start(bf16[2,1,128,1280]{3,2,1,0:T(8,128)(2,1)} %param.21) | copy-start | bytes 1966084
  71.2 169.8 %collective-permute-start.2 = (bf16[320,5120]{1,0:T(8,128)(2,1)}, bf16[320,5120]{1,0:T(8,128)(2,1)}, u32[]{:S(2)}, u32[]{:S(2)}) collective-permute-start(bf16[320,5120]{1,0:T(8,128)(2,1)} %maximum_select_fusion.2), channel_id=1, source_target_pairs={{0,8},{2,10},{4,12},{6,14},{8,0},{10,2},{12,4},{14,6},{16,24},{18,... | collective-permute-start | bytes 9830408 | tf_op jit(solution)/shard_map/ppermute | solution.py:17
  239.7 360.7 %copy-start.44 = (f32[1280]{0:T(1024)}, f32[1280]{0:T(1024)S(1)}, u32[]{:S(2)}) copy-start(f32[1280]{0:T(1024)S(1)} %convert_element_type.331) | copy-start | bytes 15364
  249.1 494.1 %collective-permute-start.3 = (bf16[640,5120]{1,0:T(8,128)(2,1)}, bf16[640,5120]{1,0:T(8,128)(2,1)}, u32[]{:S(2)}, u32[]{:S(2)}) collective-permute-start(bf16[640,5120]{1,0:T(8,128)(2,1)} %maximum_select_fusion.1), channel_id=1, source_target_pairs={{0,16},{2,18},{4,20},{6,22},{8,24},{10,26},{12,28},{14,30},{16,0},... | collective-permute-start | bytes 19660808 | tf_op jit(solution)/shard_map/ppermute | solution.py:17
  267.4 320.4 %copy-start.5 = (f32[128,1280]{1,0:T(8,128)}, f32[128,1280]{1,0:T(8,128)S(1)}, u32[]{:S(2)}) copy-start(f32[128,1280]{1,0:T(8,128)S(1)} %get-tuple-element.146) | copy-start | bytes 1966084
  271.4 331.1 %copy-start.10 = (f32[128,1280]{1,0:T(8,128)}, f32[128,1280]{1,0:T(8,128)S(1)}, u32[]{:S(2)}) copy-start(f32[128,1280]{1,0:T(8,128)S(1)} %get-tuple-element.150) | copy-start | bytes 1966084
  271.4 329.0 %copy-start.76 = (f32[128]{0:T(128)}, f32[128]{0:T(128)S(1)}, u32[]{:S(2)}) copy-start(f32[128]{0:T(128)S(1)} %broadcast_multiply_fusion.10) | copy-start | bytes 1540
  271.7 328.8 %copy-start.79 = (f32[128]{0:T(128)}, f32[128]{0:T(128)S(1)}, u32[]{:S(2)}) copy-start(f32[128]{0:T(128)S(1)} %add_rsqrt_fusion.2) | copy-start | bytes 1540
  837.6 242.2 %reduce-scatter.11.cloned.1.call-start = ((), (), s32[]{:S(2)}) async-start(), calls=%async_computation.12 | async-start | bytes 3481600 | tf_op jit(solution)/shard_map/reduce_scatter | solution.py:281
  932.3 230.5 %reduce-scatter.9.cloned.1.call-start = ((), (), s32[]{:S(2)}) async-start(), calls=%async_computation.11 | async-start | bytes 10444800 | tf_op jit(solution)/shard_map/reduce_scatter | solution.py:278
  982.2 322.9 %reduce-scatter.13.cloned.1.call-start = ((), (), s32[]{:S(2)}) async-start(), calls=%async_computation.13 | async-start | bytes 13926400 | tf_op jit(solution)/shard_map/reduce_scatter | solution.py:284
  1011.7 435.5 %reduce-scatter.15.cloned.1.call-start = ((), (), s32[]{:S(2)}) async-start(), calls=%async_computation.14 | async-start | bytes 13926400 | tf_op jit(solution)/shard_map/reduce_scatter | solution.py:287
  1041.8 547.0 %reduce-scatter.17.cloned.1.call-start = ((), (), s32[]{:S(2)}) async-start(), calls=%async_computation.15 | async-start | bytes 13926400 | tf_op jit(solution)/shard_map/reduce_scatter | solution.py:299
  1076.1 633.8 %all-reduce.19.cloned.1.call-start = ((), (), s32[]{:S(2)}) async-start(), calls=%async_computation.17 | async-start | bytes 9175040 | tf_op jit(solution)/shard_map/psum | solution.py:321
  (104 other events, 2237.6 us)
Sparse Core Ops, SparseCore 0:
  10.3 104.4 all-gather.7
  117.1 60.6 all-gather.9
  180.1 264.1 all-gather.11
  446.4 141.4 all-gather.13
  590.0 135.9 all-gather.15
  837.7 137.3 reduce-scatter.18
  979.4 65.8 reduce-scatter.10
  1049.5 113.2 reduce-scatter.8
  1166.9 138.1 reduce-scatter.12
  1309.6 137.5 reduce-scatter.14
  1451.3 137.4 reduce-scatter.16
  1592.5 117.3 all-reduce.18
